TPU v7x, 32 devices: a whole 2x2x4 slice. The times are simulated.
32 devices in a mesh: groups: 2 (over y), feat: 4 (over z), dp: 2 (over x), section: 2 (over core).
Axes of the slice: x: 2, y: 2, z: 4, core: 2. Of those that a mesh axis runs over, the one named last changes fastest.
Arguments:
- residuals: bfloat16 [2, 3072, 8192], P('section', ('groups', 'dp'), 'feat'), parts along dimension 1, may hold values from -6 to 6
- final_resid: bfloat16 [3072, 8192], P(('groups', 'dp', 'section'), 'feat'), parts along dimension 0, may hold values from -6 to 6
- final_order: int32 [3072], P(('groups', 'dp')), parts along dimension 0, may hold values from 0 to 767, as said below
- translator: bfloat16 [2, 8192, 8192], P('section', 'dp', 'feat'), may hold values from -0.0625 to 0.0625
- bias: float32 [2, 8192], P('section', 'feat'), may hold values from -5 to 5
Outputs:
- grad_weight: bfloat16 [4, 8192, 8192], P(('groups', 'section'), 'dp', 'feat'), parts along dimension 0
- grad_bias: float32 [4, 8192], P(('groups', 'section'), 'feat'), parts along dimension 0
There are 2 independent parts, one for each index of `groups`. A program takes and returns all parts, laid end to end along the dimension named above; an argument that names none is the same for every part. Nothing has to cross between parts.
Inputs may be any that keep to these rules, and one draw needn't show every extreme that they name: Within each aligned block of 768 tokens final_order is a permutation of 0 to 767.
All inputs are finite; a program needn't handle non-finite values.
Results may differ from a plain program's by a relative error of at most 0.0058.
Values may be sent and summed in bfloat16 or wider, within the bound.
A program may use at most 192 MiB of HBM per device.

v0:
```python
import math
import jax
import jax.numpy as jnp
from jax import lax
from jax.sharding import PartitionSpec as P


def on_device(residuals, final_resid, final_order, translator, bias):
    layer_rows = residuals[0]
    local_weight = translator[0]
    gathered_final = lax.all_gather(final_resid, "section", axis=0, tiled=True)
    targets = gathered_final[final_order].astype(jnp.float32)
    full_weight = lax.all_gather(local_weight, "dp", axis=0, tiled=True)
    gathered = lax.all_gather(layer_rows, "feat", axis=1, tiled=True)
    product = jnp.dot(gathered, full_weight, preferred_element_type=jnp.float32)
    predicted = layer_rows.astype(jnp.float32) + product + bias[0]
    token_total = layer_rows.shape[0] * lax.axis_size("dp")
    factor = 1.0 / math.sqrt(token_total)
    scaled_error = (predicted - targets) * factor
    grad_b = lax.psum(jnp.sum(scaled_error, axis=0), "dp")
    rounded = scaled_error.astype(jnp.bfloat16)
    partial_sum = lax.dot_general(
        gathered, rounded, (((0,), (0,)), ((), ())), preferred_element_type=jnp.float32
    )
    partial_sum = lax.optimization_barrier(partial_sum.astype(jnp.bfloat16))
    grad_w = lax.psum_scatter(
        partial_sum.astype(jnp.float32).astype(jnp.bfloat16), "dp", scatter_dimension=0, tiled=True
    )
    return (grad_w[None], grad_b[None])


def solution(mesh):
    placed = (
        P("section", ("groups", "dp"), "feat"),
        P(("groups", "dp", "section"), "feat"),
        P(("groups", "dp")),
        P("section", "dp", "feat"),
        P("section", "feat"),
    )
    return jax.shard_map(
        on_device,
        mesh=mesh,
        in_specs=placed,
        out_specs=(P(("groups", "section"), "dp", "feat"), P(("groups", "section"), "feat")),
        check_vma=False,
    )
```

profile of v0, /device:TPU:0, one launch (start us, length us, event | category | flops | bytes accessed | tf_op | source)
XLA Modules:
  0.0 1101.7 jit_solution(1509310580802462595)
XLA Ops:
  7.2 0.0 all-gather.6.cloned.1.call-start
  7.2 0.7 all-gather.6.cloned.1.call-update
  7.9 0.0 all-gather.8.cloned.1.call-start
  7.9 0.7 all-gather.8.cloned.1.call-update
  8.6 0.0 copy-start.1
  8.7 0.0 all-gather.10.cloned.1.call-start
  8.7 0.7 all-gather.10.cloned.1.call-update
  9.4 0.0 reduce-scatter.2.cloned.1.call-start
  9.4 0.0 copy-done.1
  9.5 0.0 copy-start
  9.5 0.0 copy-start.2
  9.5 14.9 %all-gather.6.cloned.1.call-done = bf16[768,2048]{1,0:T(8,128)(2,1)} async-done(((bf16[384,2048]{1,0:T(8,128)(2,1)}), bf16[768,2048]{1,0:T(8,128)(2,1)}) %all-gather.6.cloned.1.call-update) | async-done | bytes 3145744 | tf_op jit(solution)/shard_map/all_gather | solution.py:11
  24.4 9.4 gather_fusion
  33.8 211.6 %all-gather.8.cloned.1.call-done = bf16[1,768,8192]{2,1,0:T(8,128)(2,1)} async-done(((bf16[1,768,2048]{2,1,0:T(8,128)(2,1)}), bf16[1,768,8192]{2,1,0:T(8,128)(2,1)}) %all-gather.8.cloned.1.call-update) | async-done | bytes 12582928 | tf_op jit(solution)/shard_map/all_gather | solution.py:14
  245.4 388.3 %all-gather.10.cloned.1.call-done = bf16[1,8192,2048]{2,1,0:T(8,128)(2,1)} async-done(((bf16[1,4096,2048]{2,1,0:T(8,128)(2,1)}), bf16[1,8192,2048]{2,1,0:T(8,128)(2,1)}) %all-gather.10.cloned.1.call-update) | async-done | bytes 33554448 | tf_op jit(solution)/shard_map/all_gather | solution.py:13
  633.7 0.0 copy-done
  633.7 0.0 copy-done.2
  633.7 34.7 %fusion.12 = (f32[2048]{0:T(1024)S(1)}, bf16[768,2048]{1,0:T(8,128)(2,1)S(1)}) fusion(bf16[768,2048]{1,0:T(8,128)(2,1)} %gather_fusion, f32[2048]{0:T(1024)S(1)} %bitcast.27, bf16[1,8192,2048]{2,1,0:T(8,128)(2,1)} %all-gather.10.cloned.1.call-done, bf16[1,768,8192]{2,1,0:T(8,128)(2,1)} %all-gather.8.cloned.1.call-done, bf16[1,768,2048]{2,1,0:T(8,128)(2,1)S(1)} %copy-done), kind=kOutput, calls=%fused_computation.13 | convolution fusion | flops 25782384640 | bytes 55590912 | tf_op jit(solution)/shard_map/dot_general | solution.py:15
  668.4 35.2 %convert_bitcast_fusion = bf16[8192,2048]{0,1:T(8,128)(2,1)} fusion(bf16[1,768,8192]{2,1,0:T(8,128)(2,1)} %all-gather.8.cloned.1.call-done, bf16[768,2048]{1,0:T(8,128)(2,1)S(1)} %get-tuple-element.5), kind=kOutput, calls=%fused_computation.3 | convolution fusion | flops 25786580992 | bytes 49283072 | tf_op jit(solution)/shard_map/dot_general | solution.py:22
  703.6 0.0 reduce-scatter.2.cloned.1.call-update
  703.7 5.6 psum.7
  709.3 363.5 %reduce-scatter.2.cloned.1.call-done = bf16[4096,2048]{0,1:T(8,128)(2,1)} async-done(((bf16[8192,2048]{0,1:T(8,128)(2,1)}), bf16[4096,2048]{0,1:T(8,128)(2,1)}) %reduce-scatter.2.cloned.1.call-update) | async-done | bytes 16777232 | tf_op jit(solution)/shard_map/reduce_scatter | solution.py:26
  1072.7 22.4 %copy.7 = bf16[1,4096,2048]{2,1,0:T(8,128)(2,1)} copy(bf16[1,4096,2048]{1,2,0:T(8,128)(2,1)} %bitcast.25) | data formatting | bytes 33554432
  (2 shorter events, 0.0 us)
Async XLA Ops:
  7.2 17.2 %all-gather.6.cloned.1.call-start = ((), (), s32[]{:S(2)}) async-start(), calls=%async_computation.1 | async-start | bytes 4718592 | tf_op jit(solution)/shard_map/all_gather | solution.py:11
  7.9 237.5 %all-gather.8.cloned.1.call-start = ((), (), s32[]{:S(2)}) async-start(), calls=%async_computation.3 | async-start | bytes 15728640 | tf_op jit(solution)/shard_map/all_gather | solution.py:14
  8.6 0.8 copy-start.1
  8.7 625.1 %all-gather.10.cloned.1.call-start = ((), (), s32[]{:S(2)}) async-start(), calls=%async_computation.4 | async-start | bytes 50331648 | tf_op jit(solution)/shard_map/all_gather | solution.py:13
  9.4 1063.3 %reduce-scatter.2.cloned.1.call-start = ((), (), s32[]{:S(2)}) async-start(), calls=%async_computation.2 | async-start | bytes 50331648 | tf_op jit(solution)/shard_map/reduce_scatter | solution.py:26
  9.5 624.2 %copy-start = (bf16[1,768,2048]{2,1,0:T(8,128)(2,1)S(1)}, bf16[1,768,2048]{2,1,0:T(8,128)(2,1)}, u32[]{:S(2)}) copy-start(bf16[1,768,2048]{2,1,0:T(8,128)(2,1)} %param.5) | copy-start | bytes 9437188
  9.5 624.2 %copy-start.2 = (f32[1,2048]{1,0:T(1,128)S(1)}, f32[1,2048]{1,0:T(1,128)}, u32[]{:S(2)}) copy-start(f32[1,2048]{1,0:T(1,128)} %param.9) | copy-start | bytes 24580
Sparse Core Ops, SparseCore 0:
  9.5 14.8 all-gather.5
  26.0 219.3 all-gather.7
  246.9 386.7 all-gather.9
  703.8 368.8 reduce-scatter.1
where the time goes:
time: 1100 us
  waiting for transfers between devices  980 us (89%)
  matrix products  69.9 us (6%)
  local copies, waits for them, and re-layouts  31.8 us (3%)
  between operations  13.8 us (1%)
    all_gather x1, waiting for transfers between devices, on_device(): full_weight = lax.all_gather(local_weight, 'dp', axis=0, tiled=True)  388 us
    reduce_scatter x1, waiting for transfers between devices, on_device(): lax.psum_scatter(partial_sum.astype(jnp.float32).astype(jnp.bfloat16), 'd...  363 us
    all_gather x1, waiting for transfers between devices, on_device(): gathered = lax.all_gather(layer_rows, 'feat', axis=1, tiled=True)  212 us
    dot_general x1, matrix products, on_device(): lax.dot_general(gathered, rounded, (((0,), (0,)), ((), ())), preferred_el...  35.2 us
    dot_general x1, matrix products, on_device(): product = jnp.dot(gathered, full_weight, preferred_element_type=jnp.float32)  34.7 us
    unnamed x7, local copies, waits for them, and re-layouts  22.4 us
  transfers between devices with their start and end apart: 4, of which 4 were waited for; matrix products, arithmetic and copies ran while one was open for 1% of the time, Pallas kernels for 0%

commit v1 on v0

--- a/solution.py
+++ b/solution.py
@@ -11,7 +11,12 @@
     gathered_final = lax.all_gather(final_resid, "section", axis=0, tiled=True)
     targets = gathered_final[final_order].astype(jnp.float32)
     full_weight = lax.all_gather(local_weight, "dp", axis=0, tiled=True)
-    gathered = lax.all_gather(layer_rows, "feat", axis=1, tiled=True)
+    ring = [layer_rows]
+    for hop in range(3):
+        ring.append(lax.ppermute(ring[-1], "feat", [(dev, (dev + 1) % 4) for dev in range(4)]))
+    gathered = jnp.roll(
+        jnp.concatenate(ring[::-1], axis=1), (lax.axis_index("feat") + 1) * ring[0].shape[1], axis=1
+    )
     product = jnp.dot(gathered, full_weight, preferred_element_type=jnp.float32)
     predicted = layer_rows.astype(jnp.float32) + product + bias[0]
     token_total = layer_rows.shape[0] * lax.axis_size("dp")

time: 1100 us -> 861 us (0.78)
  waiting for transfers between devices: 980 us -> 734 us
    all_gather x1, waiting for transfers between devices: 388 us -> 167 us  [on_device(): full_weight = lax.all_gather(local_weight, 'dp', axis=0, tiled=True)]
    all_gather x1 -> x0, waiting for transfers between devices: 212 us -> none  [on_device(): gathered = lax.all_gather(layer_rows, 'feat', axis=1, tiled=True)]
    ppermute x0 -> x3, waiting for transfers between devices: none -> 202 us  [on_device(): lax.ppermute(ring[-1], 'feat', [(dev, (dev + 1) % 4) for dev in range(4)])]
    all_gather x1, waiting for transfers between devices: 14.9 us -> 0.02 us  [on_device(): gathered_final = lax.all_gather(final_resid, 'section', axis=0, tiled=True)]
    unnamed x7 -> x17, local copies, waits for them, and re-layouts: 22.4 us -> 23.6 us
  transfers between devices with their start and end apart: 4 -> 6, of which waited for: 4 -> 5; matrix products, arithmetic and copies ran while one was open for 1% -> 4% of each run, Pallas kernels for 0% -> 0%
where the time goes in v1:
time: 861 us
  waiting for transfers between devices  734 us (85%)
  matrix products  69.7 us (8%)
  local copies, waits for them, and re-layouts  34.9 us (4%)
  between operations  13.8 us (2%)
    reduce_scatter x1, waiting for transfers between devices, on_device(): lax.psum_scatter(partial_sum.astype(jnp.float32).astype(jnp.bfloat16), 'd...  363 us
    ppermute x3, waiting for transfers between devices, on_device(): lax.ppermute(ring[-1], 'feat', [(dev, (dev + 1) % 4) for dev in range(4)])  202 us
    all_gather x1, waiting for transfers between devices, on_device(): full_weight = lax.all_gather(local_weight, 'dp', axis=0, tiled=True)  167 us
    dot_general x1, matrix products, on_device(): lax.dot_general(gathered, rounded, (((0,), (0,)), ((), ())), preferred_el...  35 us
    dot_general x1, matrix products, on_device(): product = jnp.dot(gathered, full_weight, preferred_element_type=jnp.float32)  34.7 us
    unnamed x17, local copies, waits for them, and re-layouts  23.6 us
  transfers between devices with their start and end apart: 6, of which 5 were waited for; matrix products, arithmetic and copies ran while one was open for 4% of the time, Pallas kernels for 0%

profile of v1, /device:TPU:0, one launch (start us, length us, event | category | flops | bytes accessed | tf_op | source)
XLA Modules:
  0.0 861.1 jit_solution(16034260441950724348)
XLA Ops:
  7.2 0.0 copy-start
  7.2 0.0 copy-start.3
  7.2 0.0 all-gather.4.cloned.1.call-start
  7.2 0.7 all-gather.4.cloned.1.call-update
  7.9 0.0 all-gather.6.cloned.1.call-start
  8.0 0.7 all-gather.6.cloned.1.call-update
  8.7 0.0 reduce-scatter.2.cloned.1.call-start
  8.7 0.3 copy-done
  9.1 3.0 collective-permute-start
  12.1 70.1 %collective-permute-done = bf16[768,2048]{1,0:T(8,128)(2,1)S(1)} collective-permute-done((bf16[768,2048]{1,0:T(8,128)(2,1)S(1)}, bf16[768,2048]{1,0:T(8,128)(2,1)S(1)}, u32[]{:S(2)}, u32[]{:S(2)}) %collective-permute-start) | collective-permute-done | bytes 3145760 | tf_op jit(solution)/shard_map/ppermute | solution.py:16
  82.2 0.0 copy-start.1
  82.2 1.7 copy-done.1
  83.9 0.0 collective-permute-start.1
  83.9 71.2 %collective-permute-done.1 = bf16[768,2048]{1,0:T(8,128)(2,1)} collective-permute-done((bf16[768,2048]{1,0:T(8,128)(2,1)S(1)}, bf16[768,2048]{1,0:T(8,128)(2,1)}, u32[]{:S(2)}, u32[]{:S(2)}) %collective-permute-start.1) | collective-permute-done | bytes 3145760 | tf_op jit(solution)/shard_map/ppermute | solution.py:16
  155.1 0.0 collective-permute-start.2
  155.1 0.0 copy-done.3
  155.1 0.0 all-gather.4.cloned.1.call-done
  155.1 9.4 %gather_fusion = bf16[768,2048]{1,0:T(8,128)(2,1)} fusion(bf16[768,2048]{1,0:T(8,128)(2,1)} %all-gather.4.cloned.1.call-done, s32[1024]{0:T(1024)S(1)} %pad_clamp_fusion), kind=kCustom, calls=%fused_computation | custom fusion | bytes 6294528 | tf_op jit(solution)/shard_map/gather | solution.py:12
  164.5 0.0 copy-start.2
  164.5 61.0 %collective-permute-done.2 = bf16[768,2048]{1,0:T(8,128)(2,1)} collective-permute-done((bf16[768,2048]{1,0:T(8,128)(2,1)}, bf16[768,2048]{1,0:T(8,128)(2,1)}, u32[]{:S(2)}, u32[]{:S(2)}) %collective-permute-start.2) | collective-permute-done | bytes 3145760 | tf_op jit(solution)/shard_map/ppermute | solution.py:16
  225.5 3.9 constant_dynamic-update-slice_fusion.7
  229.4 3.9 constant_dynamic-update-slice_fusion.6
  233.3 0.0 copy-done.2
  233.3 2.0 constant_dynamic-update-slice_fusion.5
  235.3 2.0 constant_dynamic-update-slice_fusion.4
  237.3 0.0 copy-start.4
  237.3 3.9 constant_dynamic-update-slice_fusion.3
  241.2 3.9 constant_dynamic-update-slice_fusion.2
  245.1 2.0 constant_dynamic-update-slice_fusion.1
  247.1 2.0 constant_dynamic-update-slice_fusion
  249.1 166.7 %all-gather.6.cloned.1.call-done = bf16[1,8192,2048]{2,1,0:T(8,128)(2,1)} async-done(((bf16[1,4096,2048]{2,1,0:T(8,128)(2,1)}), bf16[1,8192,2048]{2,1,0:T(8,128)(2,1)}) %all-gather.6.cloned.1.call-update) | async-done | bytes 33554448 | tf_op jit(solution)/shard_map/all_gather | solution.py:13
  415.7 0.0 copy-done.4
  415.7 34.7 %fusion.11 = (f32[2048]{0:T(1024)S(1)}, bf16[768,2048]{1,0:T(8,128)(2,1)S(1)}) fusion(bf16[768,2048]{1,0:T(8,128)(2,1)} %gather_fusion, f32[2048]{0:T(1024)S(1)} %bitcast.18, bf16[1,8192,2048]{2,1,0:T(8,128)(2,1)} %all-gather.6.cloned.1.call-done, bf16[768,16384]{1,0:T(8,128)(2,1)} %constant_dynamic-update-slice_fusion, s32[]{:T(128)S(6)} %select_n.17, ...), kind=kOutput, calls=%fused_computation.20 | convolution fusion | flops 25782384640 | bytes 55590916 | tf_op jit(solution)/shard_map/dot_general | solution.py:20
  450.4 35.0 %convolution_convert_fusion = bf16[8192,2048]{1,0:T(8,128)(2,1)} fusion(bf16[768,16384]{1,0:T(8,128)(2,1)} %constant_dynamic-update-slice_fusion, s32[]{:T(128)S(6)} %select_n.17, bf16[768,2048]{1,0:T(8,128)(2,1)S(1)} %get-tuple-element.3), kind=kOutput, calls=%fused_computation.3 | convolution fusion | flops 25786580992 | bytes 49283076 | tf_op jit(solution)/shard_map/dot_general | solution.py:27
  485.5 0.0 reduce-scatter.2.cloned.1.call-update
  485.5 5.6 psum.7
  491.1 363.5 %reduce-scatter.2.cloned.1.call-done = bf16[4096,2048]{1,0:T(8,128)(2,1)} async-done(((bf16[8192,2048]{1,0:T(8,128)(2,1)}), bf16[4096,2048]{1,0:T(8,128)(2,1)}) %reduce-scatter.2.cloned.1.call-update) | async-done | bytes 16777232 | tf_op jit(solution)/shard_map/reduce_scatter | solution.py:31
  (2 shorter events, 0.0 us)
Async XLA Ops:
  7.2 1.9 copy-start
  7.2 147.9 %copy-start.3 = (s32[768]{0:T(1024)S(1)}, s32[768]{0:T(1024)}, u32[]{:S(2)}) copy-start(s32[768]{0:T(1024)} %param.7) | copy-start | bytes 9220
  7.2 147.9 %all-gather.4.cloned.1.call-start = ((), (), s32[]{:S(2)}) async-start(), calls=%async_computation.1 | async-start | bytes 4718592 | tf_op jit(solution)/shard_map/all_gather | solution.py:11
  7.9 407.8 %all-gather.6.cloned.1.call-start = ((), (), s32[]{:S(2)}) async-start(), calls=%async_computation.3 | async-start | bytes 50331648 | tf_op jit(solution)/shard_map/all_gather | solution.py:13
  8.7 845.9 %reduce-scatter.2.cloned.1.call-start = ((), (), s32[]{:S(2)}) async-start(), calls=%async_computation.2 | async-start | bytes 50331648 | tf_op jit(solution)/shard_map/reduce_scatter | solution.py:31
  9.1 73.1 %collective-permute-start = (bf16[768,2048]{1,0:T(8,128)(2,1)S(1)}, bf16[768,2048]{1,0:T(8,128)(2,1)S(1)}, u32[]{:S(2)}, u32[]{:S(2)}) collective-permute-start(bf16[768,2048]{1,0:T(8,128)(2,1)S(1)} %bitcast.15), channel_id=1, source_target_pairs={{0,4},{4,8},{8,12},{12,0},{1,5},{5,9},{9,13},{13,1},{2,6},{6,10},{... | collective-permute-start | bytes 9437192 | tf_op jit(solution)/shard_map/ppermute | solution.py:16
  82.2 1.7 copy-start.1
  83.9 71.2 %collective-permute-start.1 = (bf16[768,2048]{1,0:T(8,128)(2,1)S(1)}, bf16[768,2048]{1,0:T(8,128)(2,1)}, u32[]{:S(2)}, u32[]{:S(2)}) collective-permute-start(bf16[768,2048]{1,0:T(8,128)(2,1)S(1)} %collective-permute-done), channel_id=1, source_target_pairs={{0,4},{4,8},{8,12},{12,0},{1,5},{5,9},{9,13},{13,1},{2,6},{6,10},{... | collective-permute-start | bytes 9437192 | tf_op jit(solution)/shard_map/ppermute | solution.py:16
  155.1 70.5 %collective-permute-start.2 = (bf16[768,2048]{1,0:T(8,128)(2,1)}, bf16[768,2048]{1,0:T(8,128)(2,1)}, u32[]{:S(2)}, u32[]{:S(2)}) collective-permute-start(bf16[768,2048]{1,0:T(8,128)(2,1)} %collective-permute-done.1), channel_id=1, source_target_pairs={{0,4},{4,8},{8,12},{12,0},{1,5},{5,9},{9,13},{13,1},{2,6},{6,10},{... | collective-permute-start | bytes 9437192 | tf_op jit(solution)/shard_map/ppermute | solution.py:16
  164.5 68.8 %copy-start.2 = (bf16[768,2048]{1,0:T(8,128)(2,1)S(1)}, bf16[768,2048]{1,0:T(8,128)(2,1)}, u32[]{:S(2)}) copy-start(bf16[768,2048]{1,0:T(8,128)(2,1)} %copy-done.1) | copy-start | bytes 9437188
  237.3 178.4 %copy-start.4 = (f32[1,2048]{1,0:T(1,128)S(1)}, f32[1,2048]{1,0:T(1,128)}, u32[]{:S(2)}) copy-start(f32[1,2048]{1,0:T(1,128)} %param.9) | copy-start | bytes 24580
Sparse Core Ops, SparseCore 0:
  9.6 14.8 all-gather.3
  26.0 389.7 all-gather.5
  485.6 368.8 reduce-scatter.1
